TPU v7x, 32 devices: a whole 2x2x4 slice. The times are simulated.
32 devices in a mesh: group: 2 (over y), ctx: 4 (over z), head: 4 (over x, core).
Axes of the slice: x: 2, y: 2, z: 4, core: 2. Of those that a mesh axis runs over, the one named last changes fastest.
Arguments:
- mixer_x: bfloat16 [2048, 8192], P(('group', 'ctx'), 'head'), parts along dimension 0, may hold values from -6 to 6
- mixer_bc: bfloat16 [2, 2048, 1024], P(None, ('group', 'ctx'), 'head'), parts along dimension 1, may hold values from -3 to 3
- mixer_gate: bfloat16 [2048, 8192], P(('group', 'ctx'), 'head'), parts along dimension 0, may hold values from -9 to 9
- step_logits: float32 [2048, 128], P(('group', 'ctx'), 'head'), parts along dimension 0, may hold values from -3 to 3
- conv_x_weight: float32 [4, 8192], P(None, 'head'), may hold values from -0.6 to 0.6
- conv_bc_weight: float32 [2, 4, 1024], P(None, None, 'head'), may hold values from -0.6 to 0.6
- head_params: float32 [3, 128], P(None, 'head'), as said below
- norm_gain: float32 [8192], P('head'), may hold values from 0.5 to 1.5
- grad_output: bfloat16 [2048, 8192], P(('group', 'ctx'), 'head'), parts along dimension 0, may hold values from -9 to 9
Outputs:
- grad_x: bfloat16 [2048, 8192], P(('group', 'ctx'), 'head'), parts along dimension 0
- grad_bc: bfloat16 [2, 2048, 1024], P(None, ('group', 'ctx'), 'head'), parts along dimension 1
- grad_gate: bfloat16 [2048, 8192], P(('group', 'ctx'), 'head'), parts along dimension 0
- grad_step: float32 [2048, 128], P(('group', 'ctx'), 'head'), parts along dimension 0
- grad_conv_x: float32 [8, 8192], P('group', 'head'), parts along dimension 0
- grad_conv_bc: float32 [4, 4, 1024], P('group', None, 'head'), parts along dimension 0
- grad_heads: float32 [6, 128], P('group', 'head'), parts along dimension 0
- grad_gain: float32 [16384], P(('group', 'head')), parts along dimension 0
There are 2 independent parts, one for each index of `group`. A program takes and returns all parts, laid end to end along the dimension named above; an argument that names none is the same for every part. Nothing has to cross between parts.
Inputs may be any that keep to these rules, and one draw needn't show every extreme that they name: `head_params`: row 0 is added to the step logits and lies between -1 and 1; row 1 is the logarithm of a decay rate between log(0.2 / 1024) and log(0.1); row 2 is a skip factor between 0.5 and 1.5.
All inputs are finite; a program needn't handle non-finite values.
Results may differ from a plain program's by a relative error of at most 0.014.
Values may be sent and summed in bfloat16 or wider, within the bound.
A program may use at most 128 MiB of HBM per device.

v0:
```python
import jax
import jax.numpy as jnp
from jax import lax
from jax.sharding import PartitionSpec as P

HEADS = 128
HEAD_DIM = 64
STATE = 128
GROUPS = 8
CONV = 4
SPAN = 256
INNER = 8192
epsilon = 1e-05


def passed_along(shard, axis, by):
    size = lax.axis_size(axis)
    pairs = [(i, i + by) for i in range(size) if 0 <= i + by < size]
    return lax.ppermute(shard, axis, pairs)


def entering_2(shard, axis, combine, identity):
    size, position = (lax.axis_size(axis), lax.axis_index(axis))
    everything = jax.tree.map(
        lambda part, kind: lax.all_gather(part.astype(kind), axis),
        shard,
        (jnp.bfloat16, jnp.bfloat16),
    )
    start = jax.tree.map(
        lambda part, zero: jnp.broadcast_to(jnp.asarray(zero, part.dtype), part.shape),
        shard,
        identity,
    )

    def entering_step(k, before):
        reached = k < position
        new = combine(
            before, jax.tree.map(lambda part, own: part[k].astype(own.dtype), everything, shard)
        )
        return jax.tree.map(lambda a, b: jnp.where(reached, a, b), new, before)

    return lax.fori_loop(0, size, entering_step, start)


def prefix(shard, axis, combine, identity):
    size, position = (lax.axis_size(axis), lax.axis_index(axis))
    everything = jax.tree.map(
        lambda part, kind: lax.all_gather(part.astype(kind), axis),
        shard,
        jax.tree.map(lambda a: jnp.bfloat16 if a.dtype == jnp.float32 else a.dtype, shard),
    )
    start = jax.tree.map(
        lambda part, zero: jnp.broadcast_to(jnp.asarray(zero, part.dtype), part.shape),
        shard,
        identity,
    )

    def prefix_step(k, before):
        at = size - 1 - k
        reached = at > position
        new = combine(
            before, jax.tree.map(lambda part, own: part[at].astype(own.dtype), everything, shard)
        )
        return jax.tree.map(lambda a, b: jnp.where(reached, a, b), new, before)

    return lax.fori_loop(0, size, prefix_step, start)


def conv_silu(padded_rows, kernel):
    taps_count = kernel.shape[0]
    out_rows = padded_rows.shape[0] - taps_count + 1
    summed = kernel[0] * padded_rows[0:out_rows]
    for offset in range(1, taps_count):
        summed = summed + kernel[offset] * padded_rows[offset : offset + out_rows]
    return jax.nn.silu(summed).astype(jnp.bfloat16)


def span_parts(x_block, b_block, c_block, step_block, decay_rate, skip_gain):
    log_decay = jnp.cumsum(step_block * decay_rate, axis=0)
    block_end = log_decay[-1]
    scores = jnp.einsum("tgn,sgn->gts", c_block, b_block, preferred_element_type=jnp.float32)
    by_head = jnp.transpose(log_decay, (1, 2, 0))
    spread = by_head[:, :, :, None] - by_head[:, :, None, :]
    positions = jnp.arange(log_decay.shape[0])
    causal = positions[:, None] >= positions[None, :]
    weights = jnp.where(causal, jnp.exp(jnp.where(causal, spread, 0.0)), 0.0)
    step_heads = jnp.transpose(step_block, (1, 2, 0))
    mixing = (scores[:, None] * weights * step_heads[:, :, None, :]).astype(jnp.bfloat16)
    inside = jnp.einsum("gkts,sgkp->tgkp", mixing, x_block, preferred_element_type=jnp.float32)
    inside = inside + skip_gain[None, :, :, None] * x_block.astype(jnp.float32)
    carry_weight = jnp.exp(block_end[None] - log_decay) * step_block
    scaled_x = (x_block.astype(jnp.float32) * carry_weight[..., None]).astype(jnp.bfloat16)
    block_state = jnp.einsum(
        "sgkp,sgn->gkpn", scaled_x, b_block, preferred_element_type=jnp.float32
    )
    return (inside, block_state, block_end, log_decay)


def state_read(c_block, state_low, log_decay):
    readout = jnp.einsum("tgn,gkpn->tgkp", c_block, state_low, preferred_element_type=jnp.float32)
    return readout * jnp.exp(log_decay)[..., None]


def join_states(earlier, later):
    return (earlier[0] + later[0], jnp.exp(later[0])[..., None, None] * earlier[1] + later[1])


def shards(
    mixer_x,
    mixer_bc,
    mixer_gate,
    step_logits,
    conv_x_weight,
    conv_bc_weight,
    head_params,
    norm_gain,
    grad_output,
):
    margin = CONV - 1
    length_dev = mixer_x.shape[0]
    width_dev = mixer_x.shape[1]
    columns = mixer_bc.shape[2]
    groups = columns // STATE
    per_group = HEADS // GROUPS
    blocks = length_dev // SPAN
    rim_rows = jnp.concatenate(
        [
            mixer_x[length_dev - margin :],
            mixer_bc[0, length_dev - margin :],
            mixer_bc[1, length_dev - margin :],
        ],
        axis=1,
    )
    before = passed_along(rim_rows, "ctx", 1)

    def prepare(x_own, bc_own, borrowed, step_own, conv_x, conv_bc, params_own):
        x_rows = jnp.concatenate([borrowed[:, :width_dev], x_own], axis=0)
        b_rows = jnp.concatenate([borrowed[:, width_dev : width_dev + columns], bc_own[0]], axis=0)
        c_rows = jnp.concatenate([borrowed[:, width_dev + columns :], bc_own[1]], axis=0)
        x_conv = conv_silu(x_rows, conv_x)
        b_conv = conv_silu(b_rows, conv_bc[0])
        c_conv = conv_silu(c_rows, conv_bc[1])
        step_size = jax.nn.softplus(step_own + params_own[0])
        decay_rate = (-jnp.exp(params_own[1])).reshape(groups, per_group)
        skip_gain = params_own[2].reshape(groups, per_group)
        x_blocks = x_conv.reshape(blocks, SPAN, groups, per_group, HEAD_DIM)
        b_blocks = b_conv.reshape(blocks, SPAN, groups, STATE)
        c_blocks = c_conv.reshape(blocks, SPAN, groups, STATE)
        step_blocks = step_size.reshape(blocks, SPAN, groups, per_group)
        inside_all, block_states, block_ends, log_decays = jax.vmap(
            span_parts, in_axes=(0, 0, 0, 0, None, None)
        )(x_blocks, b_blocks, c_blocks, step_blocks, decay_rate, skip_gain)
        return (inside_all, block_states, block_ends, log_decays, c_blocks)

    primals = (
        mixer_x.astype(jnp.float32),
        mixer_bc.astype(jnp.float32),
        before.astype(jnp.float32),
        step_logits,
        conv_x_weight,
        conv_bc_weight,
        head_params,
    )
    prepared, pull_prepare = jax.vjp(prepare, *primals)
    inside_all, block_states, block_ends, log_decays, c_blocks = prepared
    device_log = block_ends[0]
    device_state = block_states[0]
    empty_log = jnp.zeros_like(device_log)
    empty_state = jnp.zeros_like(device_state)
    halfway = per_group // 2
    lower_half = entering_2(
        (device_log[:, :halfway], device_state[:, :halfway]),
        "ctx",
        join_states,
        (empty_log[:, :halfway], empty_state[:, :halfway]),
    )
    upper_half = entering_2(
        (device_log[:, halfway:], device_state[:, halfway:]),
        "ctx",
        join_states,
        (empty_log[:, halfway:], empty_state[:, halfway:]),
    )
    carried = jnp.concatenate([lower_half[1], upper_half[1]], axis=1)
    number = 0
    entering = [carried]
    entering_low = jnp.stack(entering).astype(jnp.bfloat16)

    def read_all(c_part, state_part, decay_part):
        return jax.vmap(state_read)(c_part, state_part, decay_part)

    readouts, pull_read = jax.vjp(read_all, c_blocks, entering_low, log_decays)
    mixed = (inside_all + readouts).reshape(length_dev, width_dev)
    gate_value = mixer_gate.astype(jnp.float32)
    sigmoid_z = jax.nn.sigmoid(gate_value)
    gate_act = gate_value * sigmoid_z
    gated = mixed * gate_act
    upstream = grad_output.astype(jnp.float32) * norm_gain
    own_square = jnp.sum(gated * gated, axis=1)
    square = lax.psum(own_square, "head")
    factor = lax.rsqrt(square / INNER + epsilon)
    normed = gated * factor[:, None]
    projected = lax.psum(jnp.sum(upstream * normed, axis=1), "head")
    d_gated = (upstream - normed * (projected / INNER)[:, None]) * factor[:, None]
    grad_gain_own = jnp.sum(grad_output.astype(jnp.float32) * normed, axis=0)
    d_mixed = d_gated * gate_act
    grad_gate = (d_gated * mixed * (sigmoid_z * (1.0 + gate_value * (1.0 - sigmoid_z)))).astype(
        jnp.bfloat16
    )
    grad_blocks = d_mixed.reshape(inside_all.shape)
    d_c_read, d_entering_low, d_decay_read = pull_read(grad_blocks)
    d_entering = d_entering_low.astype(jnp.float32)
    pending = jnp.zeros_like(carried)
    after_zero = [None] * blocks
    for number in reversed(range(blocks)):
        after_zero[number] = pending
        pending = d_entering[number] + jnp.exp(block_ends[number])[..., None, None] * pending
    outgoing = prefix((device_log, pending), "ctx", join_states, (empty_log, empty_state))[1]
    decay_after = jnp.zeros_like(device_log)
    grad_states = [None] * blocks
    grad_ends = [None] * blocks
    for number in reversed(range(blocks)):
        state_grad = after_zero[number] + jnp.exp(decay_after)[..., None, None] * outgoing
        grad_states[number] = state_grad
        grad_ends[number] = jnp.exp(block_ends[number]) * jnp.sum(
            state_grad * entering[number], axis=(2, 3)
        )
        decay_after = block_ends[number]
    gradients = pull_prepare(
        (grad_blocks, jnp.stack(grad_states), jnp.stack(grad_ends), d_decay_read, d_c_read)
    )
    returned = passed_along(gradients[2], "ctx", -1)
    grad_x = (
        gradients[0].at[length_dev - margin :].add(returned[:, :width_dev]).astype(jnp.bfloat16)
    )
    grad_b = (
        gradients[1][0].at[length_dev - margin :].add(returned[:, width_dev : width_dev + columns])
    )
    grad_c = gradients[1][1].at[length_dev - margin :].add(returned[:, width_dev + columns :])
    grad_bc = jnp.stack([grad_b, grad_c]).astype(jnp.bfloat16)
    totals = lax.psum((gradients[4], gradients[5], gradients[6], grad_gain_own), "ctx")
    return (grad_x, grad_bc, grad_gate, gradients[3], totals[0], totals[1], totals[2], totals[3])


def solution(mesh):
    return jax.shard_map(
        shards,
        mesh=mesh,
        in_specs=(
            P(("group", "ctx"), "head"),
            P(None, ("group", "ctx"), "head"),
            P(("group", "ctx"), "head"),
            P(("group", "ctx"), "head"),
            P(None, "head"),
            P(None, None, "head"),
            P(None, "head"),
            P("head"),
            P(("group", "ctx"), "head"),
        ),
        out_specs=(
            P(("group", "ctx"), "head"),
            P(None, ("group", "ctx"), "head"),
            P(("group", "ctx"), "head"),
            P(("group", "ctx"), "head"),
            P("group", "head"),
            P("group", None, "head"),
            P("group", "head"),
            P(("group", "head")),
        ),
        check_vma=False,
    )
```

profile of v0, /device:TPU:0, one launch (start us, length us, event | category | flops | bytes accessed | tf_op | source)
XLA Modules:
  0.0 249.9 jit_solution(2895747203639951558)
XLA Ops:
  8.7 5.0 %collective-permute-start = (bf16[3,2560]{1,0:T(4,128)(2,1)S(1)}, bf16[3,2560]{1,0:T(4,128)(2,1)S(1)}, u32[]{:S(2)}, u32[]{:S(2)}) collective-permute-start(bf16[3,2560]{1,0:T(4,128)(2,1)S(1)} %pad_maximum_fusion.4), channel_id=1, source_target_pairs={{0,4},{4,8},{8,12},{1,5},{5,9},{9,13},{2,6},{6,10},{10,14},{3,7},{... | collective-permute-start | bytes 46088 | tf_op jit(solution)/shard_map/ppermute | solution.py:19
  27.2 6.4 %multiply_convert_fusion.5 = (bf16[256,2048]{0,1:T(8,128)(2,1)S(1)}, f32[256,2048]{0,1:T(8,128)}) fusion(f32[256,2048]{0,1:T(8,128)S(1)} %convert_element_type.286, f32[2048]{0:T(1024)S(1)} %bitcast.392, f32[3,2048]{0,1:T(8,128)} %copy.222, f32[2048]{0:T(1024)S(1)} %bitcast.394, f32[2048]{0:T(1024)S(1)} %bitcast.396, f32[2048]{0:T(1024)S(1)} %bitcast.390), kind=kLoop, calls=%fused_computation.81 | loop fusion | flops 7864320 | bytes 5300224 | tf_op jit(solution)/shard_map/jvp()/convert_element_type | solution.py:75
  33.7 1.7 multiply_convert_fusion.16
  37.4 9.1 %all-gather.7 = bf16[4,2,8]{2,1,0:T(2,128)(2,1)S(1)} all-gather(bf16[1,2,8]{2,1,0:T(2,128)(2,1)S(1)} %get-tuple-element.588), channel_id=5, replica_groups=mesh['group'=2,'ctx'=4,'head'=4] {'ctx'}, dimensions={0}, use_global_device_ids=true | all-gather | bytes 160 | tf_op jit(solution)/shard_map/all_gather | solution.py:25
  46.5 8.5 %all-gather.6 = bf16[4,2,8]{2,1,0:T(2,128)(2,1)S(1)} all-gather(bf16[1,2,8]{2,1,0:T(2,128)(2,1)S(1)} %get-tuple-element.589), channel_id=3, replica_groups=mesh['group'=2,'ctx'=4,'head'=4] {'ctx'}, dimensions={0}, use_global_device_ids=true | all-gather | bytes 160 | tf_op jit(solution)/shard_map/all_gather | solution.py:25
  57.1 2.3 copy.235
  59.4 2.3 copy.220
  65.1 4.5 %while.48 = (s32[]{:T(128)}, f32[2,8,64,128]{3,2,1,0:T(8,128)S(1)}, s32[]{:T(128)}, bf16[4,2,8]{2,1,0:T(2,128)(2,1)S(1)}, bf16[4,2,8,64,128]{4,3,2,1,0:T(8,128)(2,1)}, /*index=5*/s32[]{:T(128)}, s32[]{:T(128)}) while((s32[]{:T(128)}, f32[2,8,64,128]{3,2,1,0:T(8,128)S(1)}, s32[]{:T(128)}, bf16[4,2,8]{2,1,0:T(2,128)(2,1)S(1)}, ...), condition=%wide.region_5.6_spmd.clone, body=%wide.region_4.5_spmd.clone.sunk | while | flops 655380 | bytes 1310985 | solution.py:42
  69.6 24.5 %all-gather.12.cloned.1.call-done = bf16[8,8,64,128]{3,2,1,0:T(8,128)(2,1)} async-done(((bf16[2,8,64,128]{3,2,1,0:T(8,128)(2,1)}), bf16[8,8,64,128]{3,2,1,0:T(8,128)(2,1)}) %all-gather.12.cloned.1.call-update) | async-done | bytes 1048592 | tf_op jit(solution)/shard_map/all_gather | solution.py:25
  94.1 4.5 %while.47 = (s32[]{:T(128)}, f32[2,8,64,128]{3,2,1,0:T(8,128)S(1)}, s32[]{:T(128)}, bf16[4,2,8]{2,1,0:T(2,128)(2,1)S(1)}, bf16[4,2,8,64,128]{4,3,2,1,0:T(8,128)(2,1)}, /*index=5*/s32[]{:T(128)}, s32[]{:T(128)}) while((s32[]{:T(128)}, f32[2,8,64,128]{3,2,1,0:T(8,128)S(1)}, s32[]{:T(128)}, bf16[4,2,8]{2,1,0:T(2,128)(2,1)S(1)}, ...), condition=%wide.region_3.4_spmd.clone, body=%wide.region_2.3_spmd.clone.sunk | while | flops 655380 | bytes 1310985 | solution.py:42
  99.9 2.8 %fusion.32 = f32[1,256,2,16,64]{1,4,3,2,0:T(8,128)S(1)} fusion(f32[2,16,64,256]{3,2,1,0:T(8,128)S(1)} %fusion.95, bf16[256,2,16,64]{0,3,2,1:T(8,128)(2,1)S(1)} %bitcast.359, f32[2,16,256]{2,1,0:T(8,128)S(1)} %bitcast.386, f32[2,16,256]{2,1,0:T(8,128)S(1)} %copy-done.61, f32[2,256,256]{2,1,0:T(8,128)S(1)} %copy-done.42, pred[256,256]{1,0:T(8,128)(4,1)S(1)} %copy-done.58, ...), kind=kOutput, calls=%fused_computation.58 | convolution fusion | flops 283639808 | bytes 6979712 | tf_op jit(solution)/shard_map/jvp(vmap(gkts,sgkp->tgkp))/dot_general | solution.py:89
  104.0 6.7 %psum.42 = f32[256]{0:T(256)} all-reduce(f32[256]{0:T(256)} %multiply_reduce_fusion.5), channel_id=1, replica_groups=mesh['group'=2,'ctx'=4,'head'=4] {'head'}, use_global_device_ids=true, to_apply=%region_7.8 | all-reduce | flops 256 | bytes 2048 | tf_op jit(solution)/shard_map/psum | solution.py:199
  111.4 3.6 %fusion.20 = (f32[2048]{0:T(1024)}, f32[256]{0:T(256)}) fusion(bf16[256,2048]{0,1:T(8,128)(2,1)} %copy.220, f32[256]{0:T(256)S(1)} %add_rsqrt_fusion, bf16[256,2048]{0,1:T(8,128)(2,1)} %copy.235, f32[1,256,2,16,64]{1,4,3,2,0:T(8,128)S(1)} %fusion.32, f32[2048]{0:T(1024)} %param.28), kind=kLoop, calls=%fused_computation.44 | loop fusion | flops 6813440 | bytes 4212736 | tf_op jit(solution)/shard_map/reduce_sum | solution.py:204
  115.0 6.3 %psum.43 = f32[256]{0:T(256)S(1)} all-reduce(f32[256]{0:T(256)} %get-tuple-element.477), channel_id=1, replica_groups=mesh['group'=2,'ctx'=4,'head'=4] {'head'}, use_global_device_ids=true, to_apply=%region_9.10 | all-reduce | flops 256 | bytes 2048 | tf_op jit(solution)/shard_map/psum | solution.py:202
  121.3 4.9 %multiply_reduce_fusion = (f32[2048]{0:T(1024)}, f32[256,2048]{0,1:T(8,128)S(1)}, bf16[256,2048]{0,1:T(8,128)(2,1)}) fusion(bf16[256,2048]{0,1:T(8,128)(2,1)S(1)} %get-tuple-element.538, f32[256]{0:T(256)S(1)} %broadcast_multiply_fusion.13, f32[256]{0:T(256)} %copy-done.82, bf16[256,2048]{0,1:T(8,128)(2,1)} %copy.235, f32[1,256,2,16,64]{1,4,3,2,0:T(8,128)} %copy-done, ...), kind=kLoop, calls=%fused_computation.73 | loop fusion | flops 12056576 | bytes 8407040 | tf_op jit(solution)/shard_map/transpose(jvp(vmap()))/reduce_sum | solution.py:90
  127.4 9.9 %all-gather = bf16[4,1,2,16]{3,2,1,0:T(2,128)(2,1)} all-gather(bf16[1,1,2,16]{3,2,1,0:T(2,128)(2,1)} %get-tuple-element.567), channel_id=2, replica_groups=mesh['group'=2,'ctx'=4,'head'=4] {'ctx'}, dimensions={0}, use_global_device_ids=true | all-gather | bytes 320 | tf_op jit(solution)/shard_map/all_gather | solution.py:48
  137.4 2.6 %fusion.33 = f32[256,2,16]{0,2,1:T(8,128)} fusion(f32[1,256,2,16,64]{1,4,3,2,0:T(8,128)S(1)} %bitcast.353, f32[2,16,64,256]{3,2,1,0:T(8,128)} %copy-done.14), kind=kLoop, calls=%fused_computation.61 | loop fusion | flops 1040384 | bytes 4227072 | tf_op jit(solution)/shard_map/transpose(jvp(vmap()))/reduce_sum | solution.py:101
  141.6 8.2 %fusion.13 = (f32[2,16,256]{2,1,0:T(8,128)}, f32[2,16,256]{2,1,0:T(8,128)}, f32[2,16,256]{2,1,0:T(8,128)}, bf16[2,256,256]{2,1,0:T(8,128)(2,1)}) fusion(f32[2,16,256]{2,1,0:T(8,128)} %bitcast.385, f32[2,16,256]{2,1,0:T(8,128)} %copy.228, f32[2,256,256]{2,1,0:T(8,128)} %fusion.124, pred[256,256]{1,0:T(8,128)(4,1)} %iota_compare_fusion, ...), kind=kOutput, calls=%fused_computation.23 | convolution fusion | flops 301834240 | bytes 4161536 | tf_op jit(solution)/shard_map/transpose(jvp(vmap(gkts,sgkp->tgkp)))/dot_general | solution.py:89
  151.4 1.6 copy.248
  158.7 2.3 copy.258
  160.9 1.9 fusion.70
  165.4 6.9 %all-gather.16.cloned.1.call-done = bf16[8,16,64,128]{3,2,1,0:T(8,128)(2,1)} async-done(((bf16[2,16,64,128]{3,2,1,0:T(8,128)(2,1)}), bf16[8,16,64,128]{3,2,1,0:T(8,128)(2,1)}) %all-gather.16.cloned.1.call-update) | async-done | bytes 2097168 | tf_op jit(solution)/shard_map/all_gather | solution.py:48
  172.2 7.9 %while.49 = (s32[]{:T(128)}, f32[2,16,64,128]{3,2,1,0:T(8,128)S(1)}, s32[]{:T(128)}, bf16[4,2,16]{2,1,0:T(2,128)(2,1)}, bf16[4,2,16,64,128]{4,3,2,1,0:T(8,128)(2...) while((s32[]{:T(128)}, f32[2,16,64,128]{3,2,1,0:T(8,128)S(1)}, s32[]{:T(128)}, ...), condition=%wide.region_11.12_spmd.clone, body=%wide.region_10.11_spmd.clone.sunk | while | flops 1310760 | bytes 2621927 | solution.py:66
  180.2 2.1 multiply_reduce_fusion.6
  184.0 1.7 multiply_reduce_fusion.14
  189.2 3.3 %fusion.59 = bf16[1,256,2,16,64]{1,4,3,2,0:T(8,128)(2,1)S(1)} fusion(f32[2,16,64,256]{3,2,1,0:T(8,128)S(1)} %bitcast.356, f32[2,16,256]{2,1,0:T(8,128)S(1)} %bitcast.387, f32[2,16,256]{2,1,0:T(8,128)S(1)} %copy-done.62, f32[2,256,256]{2,1,0:T(8,128)S(1)} %copy-done.43, pred[256,256]{1,0:T(8,128)(4,1)S(1)} %copy-done.59, ...), kind=kOutput, calls=%fused_computation.96 | convolution fusion | flops 284688384 | bytes 6979712 | tf_op jit(solution)/shard_map/transpose(jvp(vmap(gkts,sgkp->tgkp)))/dot_general | solution.py:89
  192.5 4.1 %multiply_reduce_fusion.3 = (f32[2048]{0:T(1024)S(1)}, f32[2048]{0:T(1024)S(1)}, f32[2048]{0:T(1024)S(1)}, f32[2048]{0:T(1024)S(1)}, f32[256,2048]{0,1:T(8,128)S(1)}) fusion(f32[256,2048]{0,1:T(8,128)S(1)} %copy-done.2, f32[3,2048]{0,1:T(8,128)S(1)} %copy-done.10, bf16[256,2048]{0,1:T(8,128)(2,1)S(1)} %copy-done.9, f32[256,2048]{0,1:T(8,128)S(1)} %copy-done.13, ...), kind=kLoop, calls=%fused_computation.76 | loop fusion | flops 11526144 | bytes 8445952 | tf_op jit(solution)/shard_map/transpose(jvp())/reduce_sum | solution.py:74
  196.7 1.8 broadcast_multiply_fusion.3
  198.5 2.5 pad_add_fusion
  204.1 5.0 %reduce-window.16 = f32[1,16,2,2,128]{4,1,2,3,0:T(8,128)S(1)} reduce-window(f32[1,16,2,2,128]{4,1,2,3,0:T(8,128)S(1)} %copy.249, f32[]{:T(128)} %constant.188.clone.1), window={size=1x1x1x1x128 pad=0_0x0_0x0_0x0_0x0_127}, to_apply=%region_20.21 | reduce-window | flops 1040384 | bytes 65540 | tf_op jit(solution)/shard_map/reduce-window.2
  213.8 20.3 %all-reduce.35 = (f32[4,2048]{1,0:T(4,128)}, f32[2,4,256]{2,1,0:T(4,128)}, f32[3,32]{1,0:T(4,128)}, f32[2048]{0:T(1024)}) all-reduce(f32[4,2048]{1,0:T(4,128)S(1)} %pad_add_fusion.11, f32[2,4,256]{2,1,0:T(4,128)S(1)} %pad_add_fusion.12, f32[3,32]{1,0:T(4,128)S(1)} %pad_add_fusion.13, ...), channel_id=1, replica_groups=mesh['group'=2,'ctx'=4,'head'=4] {'ctx'}, use_global_device_ids=true, to_apply=%region_26.27 | all-reduce | flops 12384 | bytes 99072 | tf_op jit(solution)/shard_map/psum | solution.py:240
  238.3 3.6 %scatter-add.10 = bf16[256,2048]{0,1:T(8,128)(2,1)S(1)} dynamic-update-slice(bf16[256,2048]{0,1:T(8,128)(2,1)S(1)} %copy-done.17, bf16[3,2048]{0,1:T(8,128)(2,1)S(1)} %slice_add_fusion, s32[]{:T(128)} %constant.194.clone.1, s32[]{:T(128)} %constant.187.clone.1) | dynamic-update-slice | bytes 24580 | tf_op jit(solution)/shard_map/scatter-add | solution.py:233
  (348 shorter events, 72.4 us)
Async XLA Ops:
  7.2 57.9 %all-gather.14.cloned.1.call-start = ((), (), s32[]{:S(2)}) async-start(), calls=%async_computation.1 | async-start | bytes 1310720 | tf_op jit(solution)/shard_map/all_gather | solution.py:25
  8.7 15.2 %collective-permute-start = (bf16[3,2560]{1,0:T(4,128)(2,1)S(1)}, bf16[3,2560]{1,0:T(4,128)(2,1)S(1)}, u32[]{:S(2)}, u32[]{:S(2)}) collective-permute-start(bf16[3,2560]{1,0:T(4,128)(2,1)S(1)} %pad_maximum_fusion.4), channel_id=1, source_target_pairs={{0,4},{4,8},{8,12},{1,5},{5,9},{9,13},{2,6},{6,10},{10,14},{3,7},{... | collective-permute-start | bytes 46088 | tf_op jit(solution)/shard_map/ppermute | solution.py:19
  21.7 5.3 %copy-start.54 = (f32[1,2048]{1,0:T(1,128)}, f32[1,2048]{1,0:T(1,128)S(1)}, u32[]{:S(2)}) copy-start(f32[1,2048]{1,0:T(1,128)S(1)} %get-tuple-element.575) | copy-start | bytes 24580
  21.7 5.3 %copy-start.56 = (f32[1,2048]{1,0:T(1,128)}, f32[1,2048]{1,0:T(1,128)S(1)}, u32[]{:S(2)}) copy-start(f32[1,2048]{1,0:T(1,128)S(1)} %get-tuple-element.576) | copy-start | bytes 24580
  23.9 9.7 %copy-start.1 = (f32[256,2048]{0,1:T(8,128)}, f32[256,2048]{0,1:T(8,128)S(1)}, u32[]{:S(2)}) copy-start(f32[256,2048]{0,1:T(8,128)S(1)} %convert_element_type.286) | copy-start | bytes 6291460
  27.0 6.5 %copy-start.20 = (f32[256,256]{0,1:T(8,128)S(1)}, f32[256,256]{0,1:T(8,128)}, u32[]{:S(2)}) copy-start(f32[256,256]{0,1:T(8,128)} %get-tuple-element.555) | copy-start | bytes 786436
  27.0 6.5 %copy-start.22 = (f32[256,256]{0,1:T(8,128)S(1)}, f32[256,256]{0,1:T(8,128)}, u32[]{:S(2)}) copy-start(f32[256,256]{0,1:T(8,128)} %get-tuple-element.556) | copy-start | bytes 786436
  27.0 6.5 %copy-start.27 = (f32[3,256]{0,1:T(8,128)S(1)}, f32[3,256]{0,1:T(8,128)}, u32[]{:S(2)}) copy-start(f32[3,256]{0,1:T(8,128)} %copy.224) | copy-start | bytes 9220
  27.1 6.5 %copy-start.29 = (f32[3,256]{0,1:T(8,128)S(1)}, f32[3,256]{0,1:T(8,128)}, u32[]{:S(2)}) copy-start(f32[3,256]{0,1:T(8,128)} %copy.225) | copy-start | bytes 9220
  27.1 6.5 %copy-start.66 = (f32[1,1,256]{2,1,0:T(1,128)S(1)}, f32[1,1,256]{2,1,0:T(1,128)}, u32[]{:S(2)}) copy-start(f32[1,1,256]{2,1,0:T(1,128)} %get-tuple-element.579) | copy-start | bytes 3076
  27.1 6.5 %copy-start.68 = (f32[1,1,256]{2,1,0:T(1,128)S(1)}, f32[1,1,256]{2,1,0:T(1,128)}, u32[]{:S(2)}) copy-start(f32[1,1,256]{2,1,0:T(1,128)} %get-tuple-element.580) | copy-start | bytes 3076
  27.1 6.5 %copy-start.70 = (f32[1,1,256]{2,1,0:T(1,128)S(1)}, f32[1,1,256]{2,1,0:T(1,128)}, u32[]{:S(2)}) copy-start(f32[1,1,256]{2,1,0:T(1,128)} %get-tuple-element.585) | copy-start | bytes 3076
  27.1 6.5 %copy-start.72 = (f32[1,1,256]{2,1,0:T(1,128)S(1)}, f32[1,1,256]{2,1,0:T(1,128)}, u32[]{:S(2)}) copy-start(f32[1,1,256]{2,1,0:T(1,128)} %get-tuple-element.586) | copy-start | bytes 3076
  27.1 6.5 %copy-start.74 = (f32[1,1,256]{2,1,0:T(1,128)S(1)}, f32[1,1,256]{2,1,0:T(1,128)}, u32[]{:S(2)}) copy-start(f32[1,1,256]{2,1,0:T(1,128)} %get-tuple-element.581) | copy-start | bytes 3076
  27.1 6.5 %copy-start.76 = (f32[1,1,256]{2,1,0:T(1,128)S(1)}, f32[1,1,256]{2,1,0:T(1,128)}, u32[]{:S(2)}) copy-start(f32[1,1,256]{2,1,0:T(1,128)} %get-tuple-element.582) | copy-start | bytes 3076
  27.1 6.5 %copy-start.78 = (f32[1,1,256]{2,1,0:T(1,128)S(1)}, f32[1,1,256]{2,1,0:T(1,128)}, u32[]{:S(2)}) copy-start(f32[1,1,256]{2,1,0:T(1,128)} %get-tuple-element.583) | copy-start | bytes 3076
  27.1 6.5 %copy-start.80 = (f32[1,1,256]{2,1,0:T(1,128)S(1)}, f32[1,1,256]{2,1,0:T(1,128)}, u32[]{:S(2)}) copy-start(f32[1,1,256]{2,1,0:T(1,128)} %get-tuple-element.584) | copy-start | bytes 3076
  27.2 8.3 %copy-start.47 = (f32[256,2,16]{0,2,1:T(8,128)S(1)}, f32[256,2,16]{0,2,1:T(8,128)}, u32[]{:S(2)}) copy-start(f32[256,2,16]{0,2,1:T(8,128)} %copy.231) | copy-start | bytes 98308
  33.6 87.7 %copy-start.3 = (bf16[256,2048]{0,1:T(8,128)(2,1)}, bf16[256,2048]{0,1:T(8,128)(2,1)S(1)}, u32[]{:S(2)}) copy-start(bf16[256,2048]{0,1:T(8,128)(2,1)S(1)} %get-tuple-element.538) | copy-start | bytes 3145732
  35.4 27.5 %copy-start.24 = (bf16[256,256]{0,1:T(8,128)(2,1)}, bf16[256,256]{0,1:T(8,128)(2,1)S(1)}, u32[]{:S(2)}) copy-start(bf16[256,256]{0,1:T(8,128)(2,1)S(1)} %get-tuple-element.540) | copy-start | bytes 393220
  35.4 20.3 %copy-start.32 = (f32[256,2,16]{2,1,0:T(2,128)S(1)}, f32[256,2,16]{2,1,0:T(2,128)}, u32[]{:S(2)}) copy-start(f32[256,2,16]{2,1,0:T(2,128)} %get-tuple-element.536) | copy-start | bytes 98308
  35.4 21.0 %copy-start.99 = (f32[32]{0:T(128)S(1)}, f32[32]{0:T(128)}, u32[]{:S(2)}) copy-start(f32[32]{0:T(128)} %get-tuple-element.493) | copy-start | bytes 388
  36.7 57.4 %all-gather.12.cloned.1.call-start = ((), (), s32[]{:S(2)}) async-start(), calls=%async_computation | async-start | bytes 1310720 | tf_op jit(solution)/shard_map/all_gather | solution.py:25
  62.9 109.3 %all-gather.16.cloned.1.call-start = ((), (), s32[]{:S(2)}) async-start(), calls=%async_computation.2 | async-start | bytes 2621440 | tf_op jit(solution)/shard_map/all_gather | solution.py:48
  102.7 12.3 %copy-start = (f32[1,256,2,16,64]{1,4,3,2,0:T(8,128)}, f32[1,256,2,16,64]{1,4,3,2,0:T(8,128)S(1)}, u32[]{:S(2)}) copy-start(f32[1,256,2,16,64]{1,4,3,2,0:T(8,128)S(1)} %fusion.32) | copy-start | bytes 6291460
  203.0 6.5 %copy-start.34 = (f32[2,16,256]{1,0,2:T(2,128)S(1)}, f32[2,16,256]{1,0,2:T(2,128)}, u32[]{:S(2)}) copy-start(f32[2,16,256]{1,0,2:T(2,128)} %copy.244) | copy-start | bytes 98308
  203.0 6.5 %copy-start.97 = (f32[2,16]{1,0:T(2,128)S(1)}, f32[2,16]{1,0:T(2,128)}, u32[]{:S(2)}) copy-start(f32[2,16]{1,0:T(2,128)} %copy-done.96) | copy-start | bytes 388
  203.5 6.5 %copy-start.50 = (f32[256,32]{0,1:T(8,128)S(1)}, f32[256,32]{0,1:T(8,128)}, u32[]{:S(2)}) copy-start(f32[256,32]{0,1:T(8,128)} %param.24) | copy-start | bytes 98308
  203.5 6.5 %copy-start.85 = (f32[32]{0:T(128)S(1)}, f32[32]{0:T(128)}, u32[]{:S(2)}) copy-start(f32[32]{0:T(128)} %copy-done.84) | copy-start | bytes 388
  203.5 8.2 %slice-start = ((f32[259,2048]{0,1:T(8,128)}), f32[3,2048]{0,1:T(8,128)S(1)}, s32[]{:S(2)}) async-start(f32[259,2048]{0,1:T(8,128)} %copy-done.7), calls=%async_computation.3 | async-start | bytes 2097152 | tf_op jit(solution)/shard_map/transpose(jvp())/split | solution.py:137
  203.5 8.2 %copy-start.41 = (f32[3,256]{0,1:T(8,128)S(1)}, f32[3,256]{0,1:T(8,128)}, u32[]{:S(2)}) copy-start(f32[3,256]{0,1:T(8,128)} %pad_add_fusion.9) | copy-start | bytes 9220
  212.2 21.9 %collective-permute-start.1 = (f32[3,2560]{1,0:T(4,128)S(1)}, f32[3,2560]{1,0:T(4,128)S(1)}, u32[]{:S(2)}, u32[]{:S(2)}) collective-permute-start(f32[3,2560]{1,0:T(4,128)S(1)} %copy.239), channel_id=1, source_target_pairs={{4,0},{8,4},{12,8},{5,1},{9,5},{13,9},{6,2},{10,6},{14,10},{7,3},{... | collective-permute-start | bytes 92168 | tf_op jit(solution)/shard_map/ppermute | solution.py:19
  (76 other events, 188.8 us)
Sparse Core Ops, SparseCore 0:
  36.8 28.2 all-gather.13
  66.7 27.3 all-gather.11
  127.6 44.6 all-gather.15
where the time goes:
time: 252 us; the launch traced here: 250 us
  other arithmetic  70 us (28%)
  blocking collectives  61 us (24%)
  local copies, waits for them, and re-layouts  41.1 us (16%)
  waiting for transfers between devices  32.5 us (13%)
  matrix products  23.3 us (9%)
  between operations  15.4 us (6%)
  starting transfers between devices  6.37 us (3%)
    all_gather x2, waiting for transfers between devices, entering_2(): lax.all_gather(part.astype(kind), axis)  25.6 us
    psum x1, blocking collectives, shards(): lax.psum((gradients[4], gradients[5], gradients[6], grad_gain_own), 'ctx')  20.3 us
    all_gather x2, blocking collectives, entering_2(): lax.all_gather(part.astype(kind), axis)  17.6 us
    dot_general x3, matrix products, span_parts(): jnp.einsum('gkts,sgkp->tgkp', mixing, x_block, preferred_element_type=jnp...  14.3 us
    unnamed x214, local copies, waits for them, and re-layouts  13.1 us
    all_gather x1, blocking collectives, prefix(): lax.all_gather(part.astype(kind), axis)  9.92 us
    select_n x8, other arithmetic, entering_step(): return jax.tree.map(lambda a, b: jnp.where(reached, a, b), new, before)  8.73 us
    convert_element_type x2, other arithmetic, conv_silu(): return jax.nn.silu(summed).astype(jnp.bfloat16)  8.12 us
  transfers between devices with their start and end apart: 5, of which 3 were waited for; matrix products, arithmetic and copies ran while one was open for 21% of the time, Pallas kernels for 0%

commit v1 on v0

--- a/solution.py
+++ b/solution.py
@@ -199,7 +199,7 @@
     square = lax.psum(own_square, "head")
     factor = lax.rsqrt(square / INNER + epsilon)
     normed = gated * factor[:, None]
-    projected = lax.psum(jnp.sum(upstream * normed, axis=1), "head")
+    projected = jnp.sum(lax.all_gather(jnp.sum(upstream * normed, axis=1), "head"), axis=0)
     d_gated = (upstream - normed * (projected / INNER)[:, None]) * factor[:, None]
     grad_gain_own = jnp.sum(grad_output.astype(jnp.float32) * normed, axis=0)
     d_mixed = d_gated * gate_act

time: 252 us -> 272 us (1.079)
  local copies, waits for them, and re-layouts: 41.1 us -> 51.3 us
  other arithmetic: 70 us -> 79.8 us
    psum x1 -> x0, blocking collectives: 6.33 us -> none  [shards(): projected = lax.psum(jnp.sum(upstream * normed, axis=1), 'head')]
    all_gather x0 -> x1, blocking collectives: none -> 5.23 us  [shards(): lax.all_gather(jnp.sum(upstream * normed, axis=1), 'head')]
    unnamed x214 -> x218, local copies, waits for them, and re-layouts: 13.1 us -> 15 us
  transfers between devices with their start and end apart: 5 -> 5, of which waited for: 3 -> 3; matrix products, arithmetic and copies ran while one was open for 21% -> 20% of each run, Pallas kernels for 0% -> 0%
where the time goes in v1:
time: 272 us; the launch traced here: 269 us
  other arithmetic  79.8 us (29%)
  blocking collectives  61.2 us (22%)
  local copies, waits for them, and re-layouts  51.3 us (19%)
  waiting for transfers between devices  32 us (12%)
  matrix products  23.3 us (9%)
  between operations  15.2 us (6%)
  starting transfers between devices  6.37 us (2%)
    all_gather x2, waiting for transfers between devices, entering_2(): lax.all_gather(part.astype(kind), axis)  25.6 us
    psum x1, blocking collectives, shards(): lax.psum((gradients[4], gradients[5], gradients[6], grad_gain_own), 'ctx')  20.8 us
    all_gather x2, blocking collectives, entering_2(): lax.all_gather(part.astype(kind), axis)  17.6 us
    unnamed x218, local copies, waits for them, and re-layouts  15 us
    dot_general x3, matrix products, span_parts(): jnp.einsum('gkts,sgkp->tgkp', mixing, x_block, preferred_element_type=jnp...  14.3 us
    all_gather x1, blocking collectives, prefix(): lax.all_gather(part.astype(kind), axis)  10.8 us
    select_n x8, other arithmetic, entering_step(): return jax.tree.map(lambda a, b: jnp.where(reached, a, b), new, before)  8.73 us
    convert_element_type x2, other arithmetic, conv_silu(): return jax.nn.silu(summed).astype(jnp.bfloat16)  8.1 us
  transfers between devices with their start and end apart: 5, of which 3 were waited for; matrix products, arithmetic and copies ran while one was open for 20% of the time, Pallas kernels for 0%

profile of v1, /device:TPU:0, one launch (start us, length us, event | category | flops | bytes accessed | tf_op | source)
XLA Modules:
  0.0 269.4 jit_solution(12102898184971824187)
XLA Ops:
  8.7 5.0 %collective-permute-start = (bf16[3,2560]{1,0:T(4,128)(2,1)S(1)}, bf16[3,2560]{1,0:T(4,128)(2,1)S(1)}, u32[]{:S(2)}, u32[]{:S(2)}) collective-permute-start(bf16[3,2560]{1,0:T(4,128)(2,1)S(1)} %pad_maximum_fusion.4), channel_id=1, source_target_pairs={{0,4},{4,8},{8,12},{1,5},{5,9},{9,13},{2,6},{6,10},{10,14},{3,7},{... | collective-permute-start | bytes 46088 | tf_op jit(solution)/shard_map/ppermute | solution.py:19
  27.9 6.4 %multiply_convert_fusion.5 = (bf16[256,2048]{0,1:T(8,128)(2,1)S(1)}, f32[256,2048]{0,1:T(8,128)}) fusion(f32[256,2048]{0,1:T(8,128)S(1)} %convert_element_type.286, f32[2048]{0:T(1024)S(1)} %bitcast.393, f32[3,2048]{0,1:T(8,128)} %copy.222, f32[2048]{0:T(1024)S(1)} %bitcast.395, f32[2048]{0:T(1024)S(1)} %bitcast.397, f32[2048]{0:T(1024)S(1)} %bitcast.391), kind=kLoop, calls=%fused_computation.81 | loop fusion | flops 7864320 | bytes 5300224 | tf_op jit(solution)/shard_map/jvp()/convert_element_type | solution.py:75
  38.1 9.1 %all-gather.8 = bf16[4,2,8]{2,1,0:T(2,128)(2,1)S(1)} all-gather(bf16[1,2,8]{2,1,0:T(2,128)(2,1)S(1)} %get-tuple-element.588), channel_id=5, replica_groups=mesh['group'=2,'ctx'=4,'head'=4] {'ctx'}, dimensions={0}, use_global_device_ids=true | all-gather | bytes 160 | tf_op jit(solution)/shard_map/all_gather | solution.py:25
  47.2 8.5 %all-gather.7 = bf16[4,2,8]{2,1,0:T(2,128)(2,1)S(1)} all-gather(bf16[1,2,8]{2,1,0:T(2,128)(2,1)S(1)} %get-tuple-element.589), channel_id=3, replica_groups=mesh['group'=2,'ctx'=4,'head'=4] {'ctx'}, dimensions={0}, use_global_device_ids=true | all-gather | bytes 160 | tf_op jit(solution)/shard_map/all_gather | solution.py:25
  57.8 2.3 copy.235
  60.1 2.3 copy.220
  65.8 4.5 %while.48 = (s32[]{:T(128)}, f32[2,8,64,128]{3,2,1,0:T(8,128)S(1)}, s32[]{:T(128)}, bf16[4,2,8]{2,1,0:T(2,128)(2,1)S(1)}, bf16[4,2,8,64,128]{4,3,2,1,0:T(8,128)(2,1)}, /*index=5*/s32[]{:T(128)}, s32[]{:T(128)}) while((s32[]{:T(128)}, f32[2,8,64,128]{3,2,1,0:T(8,128)S(1)}, s32[]{:T(128)}, bf16[4,2,8]{2,1,0:T(2,128)(2,1)S(1)}, ...), condition=%wide.region_5.6_spmd.clone, body=%wide.region_4.5_spmd.clone.sunk | while | flops 655380 | bytes 1310985 | solution.py:42
  70.3 24.5 %all-gather.14.cloned.1.call-done = bf16[8,8,64,128]{3,2,1,0:T(8,128)(2,1)} async-done(((bf16[2,8,64,128]{3,2,1,0:T(8,128)(2,1)}), bf16[8,8,64,128]{3,2,1,0:T(8,128)(2,1)}) %all-gather.14.cloned.1.call-update) | async-done | bytes 1048592 | tf_op jit(solution)/shard_map/all_gather | solution.py:25
  94.8 4.5 %while.47 = (s32[]{:T(128)}, f32[2,8,64,128]{3,2,1,0:T(8,128)S(1)}, s32[]{:T(128)}, bf16[4,2,8]{2,1,0:T(2,128)(2,1)S(1)}, bf16[4,2,8,64,128]{4,3,2,1,0:T(8,128)(2,1)}, /*index=5*/s32[]{:T(128)}, s32[]{:T(128)}) while((s32[]{:T(128)}, f32[2,8,64,128]{3,2,1,0:T(8,128)S(1)}, s32[]{:T(128)}, bf16[4,2,8]{2,1,0:T(2,128)(2,1)S(1)}, ...), condition=%wide.region_3.4_spmd.clone, body=%wide.region_2.3_spmd.clone.sunk | while | flops 655380 | bytes 1310985 | solution.py:42
  100.6 2.8 %fusion.32 = f32[1,256,2,16,64]{1,4,3,2,0:T(8,128)S(1)} fusion(f32[2,16,64,256]{3,2,1,0:T(8,128)S(1)} %fusion.95, bf16[256,2,16,64]{0,3,2,1:T(8,128)(2,1)S(1)} %bitcast.360, f32[2,16,256]{2,1,0:T(8,128)S(1)} %bitcast.387, f32[2,16,256]{2,1,0:T(8,128)S(1)} %copy-done.61, f32[2,256,256]{2,1,0:T(8,128)S(1)} %copy-done.39, pred[256,256]{1,0:T(8,128)(4,1)S(1)} %copy-done.54, ...), kind=kOutput, calls=%fused_computation.58 | convolution fusion | flops 283639808 | bytes 6979712 | tf_op jit(solution)/shard_map/jvp(vmap(gkts,sgkp->tgkp))/dot_general | solution.py:89
  104.7 6.7 %psum.35 = f32[256]{0:T(256)} all-reduce(f32[256]{0:T(256)} %multiply_reduce_fusion.5), channel_id=1, replica_groups=mesh['group'=2,'ctx'=4,'head'=4] {'head'}, use_global_device_ids=true, to_apply=%region_7.8 | all-reduce | flops 256 | bytes 2048 | tf_op jit(solution)/shard_map/psum | solution.py:199
  112.1 3.6 %fusion.20 = (f32[2048]{0:T(1024)}, f32[256]{0:T(256)S(1)}) fusion(bf16[256,2048]{0,1:T(8,128)(2,1)} %copy.220, f32[256]{0:T(256)S(1)} %add_rsqrt_fusion, bf16[256,2048]{0,1:T(8,128)(2,1)} %copy.235, f32[1,256,2,16,64]{1,4,3,2,0:T(8,128)S(1)} %fusion.32, f32[2048]{0:T(1024)} %param.28), kind=kLoop, calls=%fused_computation.44 | loop fusion | flops 6813440 | bytes 4212736 | tf_op jit(solution)/shard_map/reduce_sum | solution.py:204
  115.7 5.2 %all-gather.9 = f32[4,1,256]{2,1,0:T(1,128)S(1)} all-gather(f32[1,1,256]{2,1,0:T(1,128)S(1)} %bitcast.431), channel_id=7, replica_groups=mesh['group'=2,'ctx'=4,'head'=4] {'head'}, dimensions={0}, use_global_device_ids=true | all-gather | bytes 5120 | tf_op jit(solution)/shard_map/all_gather | solution.py:202
  121.0 4.8 %multiply_reduce_fusion = (f32[2048]{0:T(1024)}, f32[256,2048]{0,1:T(8,128)S(1)}, bf16[256,2048]{0,1:T(8,128)(2,1)}) fusion(bf16[256,2048]{0,1:T(8,128)(2,1)S(1)} %get-tuple-element.538, f32[256]{0:T(256)S(1)} %broadcast_multiply_fusion.13, f32[256]{0:T(256)} %copy-done.82, bf16[256,2048]{0,1:T(8,128)(2,1)} %copy.235, f32[1,256,2,16,64]{1,4,3,2,0:T(8,128)} %copy-done, ...), kind=kLoop, calls=%fused_computation.73 | loop fusion | flops 12056576 | bytes 8407040 | tf_op jit(solution)/shard_map/transpose(jvp(vmap()))/reduce_sum | solution.py:90
  127.1 10.8 %all-gather = bf16[4,1,2,16]{3,2,1,0:T(2,128)(2,1)} all-gather(bf16[1,1,2,16]{3,2,1,0:T(2,128)(2,1)} %get-tuple-element.567), channel_id=2, replica_groups=mesh['group'=2,'ctx'=4,'head'=4] {'ctx'}, dimensions={0}, use_global_device_ids=true | all-gather | bytes 320 | tf_op jit(solution)/shard_map/all_gather | solution.py:48
  137.9 2.6 fusion.33
  142.1 8.2 %fusion.13 = (f32[2,16,256]{2,1,0:T(8,128)}, f32[2,16,256]{2,1,0:T(8,128)}, f32[2,16,256]{2,1,0:T(8,128)}, bf16[2,256,256]{2,1,0:T(8,128)(2,1)}) fusion(f32[2,16,256]{2,1,0:T(8,128)} %bitcast.386, f32[2,16,256]{2,1,0:T(8,128)} %copy.228, f32[2,256,256]{2,1,0:T(8,128)} %fusion.124, pred[256,256]{1,0:T(8,128)(4,1)} %iota_compare_fusion, ...), kind=kOutput, calls=%fused_computation.23 | convolution fusion | flops 301834240 | bytes 4161536 | tf_op jit(solution)/shard_map/transpose(jvp(vmap(gkts,sgkp->tgkp)))/dot_general | solution.py:89
  159.1 2.3 copy.258
  161.3 1.9 fusion.70
  165.8 6.4 %all-gather.18.cloned.1.call-done = bf16[8,16,64,128]{3,2,1,0:T(8,128)(2,1)} async-done(((bf16[2,16,64,128]{3,2,1,0:T(8,128)(2,1)}), bf16[8,16,64,128]{3,2,1,0:T(8,128)(2,1)}) %all-gather.18.cloned.1.call-update) | async-done | bytes 2097168 | tf_op jit(solution)/shard_map/all_gather | solution.py:48
  172.1 7.7 %while.49 = (s32[]{:T(128)}, f32[2,16,64,128]{3,2,1,0:T(8,128)S(1)}, s32[]{:T(128)}, bf16[4,2,16]{2,1,0:T(2,128)(2,1)}, bf16[4,2,16,64,128]{4,3,2,1,0:T(8,128)(2...) while((s32[]{:T(128)}, f32[2,16,64,128]{3,2,1,0:T(8,128)S(1)}, s32[]{:T(128)}, ...), condition=%wide.region_11.12_spmd.clone, body=%wide.region_10.11_spmd.clone.sunk | while | flops 1310760 | bytes 2621927 | solution.py:66
  179.9 2.1 multiply_reduce_fusion.6
  188.8 3.3 %fusion.59 = bf16[1,256,2,16,64]{1,4,3,2,0:T(8,128)(2,1)S(1)} fusion(f32[2,16,64,256]{3,2,1,0:T(8,128)S(1)} %bitcast.357, f32[2,16,256]{2,1,0:T(8,128)S(1)} %bitcast.388, f32[2,16,256]{2,1,0:T(8,128)S(1)} %copy-done.62, f32[2,256,256]{2,1,0:T(8,128)S(1)} %copy-done.40, pred[256,256]{1,0:T(8,128)(4,1)S(1)} %copy-done.55, ...), kind=kOutput, calls=%fused_computation.96 | convolution fusion | flops 284688384 | bytes 6979712 | tf_op jit(solution)/shard_map/transpose(jvp(vmap(gkts,sgkp->tgkp)))/dot_general | solution.py:89
  192.1 4.7 %multiply_reduce_fusion.3 = (f32[2048]{0:T(1024)}, f32[2048]{0:T(1024)}, f32[2048]{0:T(1024)}, f32[2048]{0:T(1024)}, f32[256,2048]{0,1:T(8,128)S(1)}) fusion(f32[256,2048]{0,1:T(8,128)S(1)} %copy-done.2, f32[3,2048]{0,1:T(8,128)S(1)} %copy-done.11, bf16[256,2048]{0,1:T(8,128)(2,1)S(1)} %copy-done.10, f32[256,2048]{0,1:T(8,128)S(1)} %copy-done.14, ...), kind=kLoop, calls=%fused_computation.76 | loop fusion | flops 11526144 | bytes 8445952 | tf_op jit(solution)/shard_map/transpose(jvp())/reduce_sum | solution.py:74
  196.9 1.8 broadcast_multiply_fusion.3
  198.7 2.5 pad_add_fusion
  205.4 1.8 fusion.89
  207.3 5.0 %reduce-window.16 = f32[1,16,2,2,128]{4,1,2,3,0:T(8,128)S(1)} reduce-window(f32[1,16,2,2,128]{4,1,2,3,0:T(8,128)S(1)} %copy.249, f32[]{:T(128)} %constant.188.clone.1), window={size=1x1x1x1x128 pad=0_0x0_0x0_0x0_0x0_127}, to_apply=%region_20.21 | reduce-window | flops 1040384 | bytes 65540 | tf_op jit(solution)/shard_map/reduce-window.2
  220.9 20.8 %all-reduce.35 = (f32[4,2048]{1,0:T(4,128)}, f32[2,4,256]{2,1,0:T(4,128)}, f32[3,32]{1,0:T(4,128)}, f32[2048]{0:T(1024)}) all-reduce(f32[4,2048]{1,0:T(4,128)S(1)} %pad_add_fusion.11, f32[2,4,256]{2,1,0:T(4,128)} %pad_add_fusion.12, f32[3,32]{1,0:T(4,128)} %pad_add_fusion.13, ...), channel_id=1, replica_groups=mesh['group'=2,'ctx'=4,'head'=4] {'ctx'}, use_global_device_ids=true, to_apply=%region_26.27 | all-reduce | flops 12384 | bytes 99072 | tf_op jit(solution)/shard_map/psum | solution.py:240
  252.4 2.1 slice_add_fusion
  254.5 6.1 %scatter-add.10 = bf16[256,2048]{0,1:T(8,128)(2,1)} dynamic-update-slice(bf16[256,2048]{0,1:T(8,128)(2,1)} %split.24, bf16[3,2048]{0,1:T(8,128)(2,1)} %slice_add_fusion, s32[]{:T(128)} %constant.194.clone.1, s32[]{:T(128)} %constant.187.clone.1) | dynamic-update-slice | bytes 24580 | tf_op jit(solution)/shard_map/scatter-add | solution.py:233
  260.6 2.3 copy.256
  (353 shorter events, 88.2 us)
Async XLA Ops:
  7.2 58.7 %all-gather.16.cloned.1.call-start = ((), (), s32[]{:S(2)}) async-start(), calls=%async_computation.1 | async-start | bytes 1310720 | tf_op jit(solution)/shard_map/all_gather | solution.py:25
  8.7 15.9 %collective-permute-start = (bf16[3,2560]{1,0:T(4,128)(2,1)S(1)}, bf16[3,2560]{1,0:T(4,128)(2,1)S(1)}, u32[]{:S(2)}, u32[]{:S(2)}) collective-permute-start(bf16[3,2560]{1,0:T(4,128)(2,1)S(1)} %pad_maximum_fusion.4), channel_id=1, source_target_pairs={{0,4},{4,8},{8,12},{1,5},{5,9},{9,13},{2,6},{6,10},{10,14},{3,7},{... | collective-permute-start | bytes 46088 | tf_op jit(solution)/shard_map/ppermute | solution.py:19
  24.6 9.7 %copy-start.1 = (f32[256,2048]{0,1:T(8,128)}, f32[256,2048]{0,1:T(8,128)S(1)}, u32[]{:S(2)}) copy-start(f32[256,2048]{0,1:T(8,128)S(1)} %convert_element_type.286) | copy-start | bytes 6291460
  27.8 6.5 %copy-start.20 = (f32[256,256]{0,1:T(8,128)S(1)}, f32[256,256]{0,1:T(8,128)}, u32[]{:S(2)}) copy-start(f32[256,256]{0,1:T(8,128)} %get-tuple-element.555) | copy-start | bytes 786436
  27.8 6.5 %copy-start.22 = (f32[256,256]{0,1:T(8,128)S(1)}, f32[256,256]{0,1:T(8,128)}, u32[]{:S(2)}) copy-start(f32[256,256]{0,1:T(8,128)} %get-tuple-element.556) | copy-start | bytes 786436
  27.8 6.5 %copy-start.27 = (f32[3,256]{0,1:T(8,128)S(1)}, f32[3,256]{0,1:T(8,128)}, u32[]{:S(2)}) copy-start(f32[3,256]{0,1:T(8,128)} %copy.224) | copy-start | bytes 9220
  27.8 6.5 %copy-start.29 = (f32[3,256]{0,1:T(8,128)S(1)}, f32[3,256]{0,1:T(8,128)}, u32[]{:S(2)}) copy-start(f32[3,256]{0,1:T(8,128)} %copy.225) | copy-start | bytes 9220
  27.8 6.5 %copy-start.66 = (f32[1,1,256]{2,1,0:T(1,128)S(1)}, f32[1,1,256]{2,1,0:T(1,128)}, u32[]{:S(2)}) copy-start(f32[1,1,256]{2,1,0:T(1,128)} %get-tuple-element.579) | copy-start | bytes 3076
  27.8 6.5 %copy-start.68 = (f32[1,1,256]{2,1,0:T(1,128)S(1)}, f32[1,1,256]{2,1,0:T(1,128)}, u32[]{:S(2)}) copy-start(f32[1,1,256]{2,1,0:T(1,128)} %get-tuple-element.580) | copy-start | bytes 3076
  27.8 6.5 %copy-start.70 = (f32[1,1,256]{2,1,0:T(1,128)S(1)}, f32[1,1,256]{2,1,0:T(1,128)}, u32[]{:S(2)}) copy-start(f32[1,1,256]{2,1,0:T(1,128)} %get-tuple-element.585) | copy-start | bytes 3076
  27.8 6.5 %copy-start.72 = (f32[1,1,256]{2,1,0:T(1,128)S(1)}, f32[1,1,256]{2,1,0:T(1,128)}, u32[]{:S(2)}) copy-start(f32[1,1,256]{2,1,0:T(1,128)} %get-tuple-element.586) | copy-start | bytes 3076
  27.9 6.5 %copy-start.74 = (f32[1,1,256]{2,1,0:T(1,128)S(1)}, f32[1,1,256]{2,1,0:T(1,128)}, u32[]{:S(2)}) copy-start(f32[1,1,256]{2,1,0:T(1,128)} %get-tuple-element.581) | copy-start | bytes 3076
  27.9 6.5 %copy-start.76 = (f32[1,1,256]{2,1,0:T(1,128)S(1)}, f32[1,1,256]{2,1,0:T(1,128)}, u32[]{:S(2)}) copy-start(f32[1,1,256]{2,1,0:T(1,128)} %get-tuple-element.582) | copy-start | bytes 3076
  27.9 6.5 %copy-start.78 = (f32[1,1,256]{2,1,0:T(1,128)S(1)}, f32[1,1,256]{2,1,0:T(1,128)}, u32[]{:S(2)}) copy-start(f32[1,1,256]{2,1,0:T(1,128)} %get-tuple-element.583) | copy-start | bytes 3076
  27.9 6.5 %copy-start.80 = (f32[1,1,256]{2,1,0:T(1,128)S(1)}, f32[1,1,256]{2,1,0:T(1,128)}, u32[]{:S(2)}) copy-start(f32[1,1,256]{2,1,0:T(1,128)} %get-tuple-element.584) | copy-start | bytes 3076
  27.9 8.2 %copy-start.44 = (f32[256,2,16]{0,2,1:T(8,128)S(1)}, f32[256,2,16]{0,2,1:T(8,128)}, u32[]{:S(2)}) copy-start(f32[256,2,16]{0,2,1:T(8,128)} %copy.231) | copy-start | bytes 98308
  34.3 86.7 %copy-start.3 = (bf16[256,2048]{0,1:T(8,128)(2,1)}, bf16[256,2048]{0,1:T(8,128)(2,1)S(1)}, u32[]{:S(2)}) copy-start(bf16[256,2048]{0,1:T(8,128)(2,1)S(1)} %get-tuple-element.538) | copy-start | bytes 3145732
  36.1 27.5 %copy-start.24 = (bf16[256,256]{0,1:T(8,128)(2,1)}, bf16[256,256]{0,1:T(8,128)(2,1)S(1)}, u32[]{:S(2)}) copy-start(bf16[256,256]{0,1:T(8,128)(2,1)S(1)} %get-tuple-element.540) | copy-start | bytes 393220
  36.1 20.3 %copy-start.32 = (f32[256,2,16]{2,1,0:T(2,128)S(1)}, f32[256,2,16]{2,1,0:T(2,128)}, u32[]{:S(2)}) copy-start(f32[256,2,16]{2,1,0:T(2,128)} %get-tuple-element.536) | copy-start | bytes 98308
  36.1 21.0 %copy-start.101 = (f32[32]{0:T(128)S(1)}, f32[32]{0:T(128)}, u32[]{:S(2)}) copy-start(f32[32]{0:T(128)} %get-tuple-element.493) | copy-start | bytes 388
  37.4 57.4 %all-gather.14.cloned.1.call-start = ((), (), s32[]{:S(2)}) async-start(), calls=%async_computation | async-start | bytes 1310720 | tf_op jit(solution)/shard_map/all_gather | solution.py:25
  63.6 108.5 %all-gather.18.cloned.1.call-start = ((), (), s32[]{:S(2)}) async-start(), calls=%async_computation.2 | async-start | bytes 2621440 | tf_op jit(solution)/shard_map/all_gather | solution.py:48
  103.4 12.3 %copy-start = (f32[1,256,2,16,64]{1,4,3,2,0:T(8,128)}, f32[1,256,2,16,64]{1,4,3,2,0:T(8,128)S(1)}, u32[]{:S(2)}) copy-start(f32[1,256,2,16,64]{1,4,3,2,0:T(8,128)S(1)} %fusion.32) | copy-start | bytes 6291460
  203.1 9.5 %copy-start.97 = (f32[2,16]{1,0:T(2,128)S(1)}, f32[2,16]{1,0:T(2,128)}, u32[]{:S(2)}) copy-start(f32[2,16]{1,0:T(2,128)} %copy-done.96) | copy-start | bytes 388
  203.1 9.5 %copy-start.13 = (f32[1,256,2,16]{3,2,1,0:T(2,128)S(1)}, f32[1,256,2,16]{3,2,1,0:T(2,128)}, u32[]{:S(2)}) copy-start(f32[1,256,2,16]{3,2,1,0:T(2,128)} %copy-done.12) | copy-start | bytes 98308
  203.1 9.5 %copy-start.34 = (f32[2,16,256]{1,0,2:T(2,128)S(1)}, f32[2,16,256]{1,0,2:T(2,128)}, u32[]{:S(2)}) copy-start(f32[2,16,256]{1,0,2:T(2,128)} %copy.244) | copy-start | bytes 98308
  205.4 7.8 %copy-start.46 = (f32[256,32]{0,1:T(8,128)S(1)}, f32[256,32]{0,1:T(8,128)}, u32[]{:S(2)}) copy-start(f32[256,32]{0,1:T(8,128)} %param.24) | copy-start | bytes 98308
  205.4 7.8 %copy-start.85 = (f32[32]{0:T(128)S(1)}, f32[32]{0:T(128)}, u32[]{:S(2)}) copy-start(f32[32]{0:T(128)} %copy-done.84) | copy-start | bytes 388
  205.4 10.6 %slice-start = ((f32[259,2048]{0,1:T(8,128)}), f32[3,2048]{0,1:T(8,128)S(1)}, s32[]{:S(2)}) async-start(f32[259,2048]{0,1:T(8,128)} %copy-done.7), calls=%async_computation.3 | async-start | bytes 2097152 | tf_op jit(solution)/shard_map/transpose(jvp())/split | solution.py:137
  205.4 10.6 %copy-start.38 = (f32[3,256]{0,1:T(8,128)S(1)}, f32[3,256]{0,1:T(8,128)}, u32[]{:S(2)}) copy-start(f32[3,256]{0,1:T(8,128)} %pad_add_fusion.9) | copy-start | bytes 9220
  216.5 25.2 %collective-permute-start.1 = (f32[3,2560]{1,0:T(4,128)S(1)}, f32[3,2560]{1,0:T(4,128)S(1)}, u32[]{:S(2)}, u32[]{:S(2)}) collective-permute-start(f32[3,2560]{1,0:T(4,128)S(1)} %copy.239), channel_id=1, source_target_pairs={{4,0},{8,4},{12,8},{5,1},{9,5},{13,9},{6,2},{10,6},{14,10},{7,3},{... | collective-permute-start | bytes 92168 | tf_op jit(solution)/shard_map/ppermute | solution.py:19
  219.3 33.1 %copy-start.8 = (f32[259,2048]{0,1:T(8,128)S(1)}, f32[259,2048]{0,1:T(8,128)}, u32[]{:S(2)}) copy-start(f32[259,2048]{0,1:T(8,128)} %copy-done.7) | copy-start | bytes 6365188
  (78 other events, 226.2 us)
Sparse Core Ops, SparseCore 0:
  37.6 28.2 all-gather.15
  67.4 27.3 all-gather.13
  127.2 44.8 all-gather.17
